TPU v7x, 128 devices: a whole 4x4x4 slice. The times are simulated.
128 devices in a mesh: pool: 16 (over x_lo, z, core), cp: 8 (over x_hi, y).
Axes of the slice: x: 4 (x_hi: 2, x_lo: 2; x = x_hi * 2 + x_lo), y: 4, z: 4, core: 2. Of those that a mesh axis runs over, the one named last changes fastest.
Arguments:
- queries: bfloat16 [16, 1024, 4096], P('pool', 'cp'), may hold values from -15 to 15
- span_keys: bfloat16 [16, 1024, 512], P('pool', 'cp'), may hold values from -6 to 6
- span_values: bfloat16 [16, 1024, 512], P('pool', 'cp'), may hold values from -6 to 6
- pool_keys: bfloat16 [384, 128, 512], P('pool'), may hold values from -6 to 6
- pool_values: bfloat16 [384, 128, 512], P('pool'), may hold values from -6 to 6
- page_ids: int32 [16, 32], replicated, may hold values from 0 to 383, as said below
- prefix_pages: int32 [16], replicated, may hold values from 1 to 32, as said below
Outputs:
- attended: float32 [16, 1024, 4096], P('pool', 'cp')
Inputs may be any that keep to these rules, and one draw needn't show every extreme that they name: `page_ids`: page p is held by index p // 24 of pool. Among the first prefix_pages[r] entries of a request, one owner holds at most 2 pages, all different; entries beyond that are unused. `prefix_pages`: some request has all 32 entries in use.
All inputs are finite; a program needn't handle non-finite values.
Results may differ from a plain program's by a relative error of at most 0.002.
Values may be sent and summed in bfloat16 or wider, within the bound.
A program may use at most 128 MiB of HBM per device.

v0:
```python
import jax
import jax.numpy as jnp
from jax import lax
from jax.sharding import PartitionSpec as P

HEAD_DIM = 128
HEADS = 32
KV_HEADS = 4
CAP = 2
PAGES_DEV = 24
NEG_FILL = -1e30


def attend(running, queries_grouped4, key_row_set, value_row_set, visible):
    total_rows = key_row_set.shape[0]
    block_len = 512
    blocks = total_rows // block_len
    score_scale = HEAD_DIM ** (-0.5)
    key_blocks = key_row_set.reshape(blocks, block_len, KV_HEADS, HEAD_DIM)
    value_blocks = value_row_set.reshape(blocks, block_len, KV_HEADS, HEAD_DIM)
    vis_blocks = visible.reshape(visible.shape[0], blocks, block_len).transpose(1, 0, 2)

    def block_step(carried, inputs):
        peak, denom, weighted_values = carried
        key_tile, value_tile, vis_block = inputs
        logit_scores = (
            jnp.einsum(
                "swxl,cwl->swxc", queries_grouped4, key_tile, preferred_element_type=jnp.float32
            )
            * score_scale
        )
        live = vis_block[:, None, None, :]
        logit_scores = jnp.where(live, logit_scores, NEG_FILL)
        new_peak = jnp.maximum(peak, jnp.max(logit_scores, axis=-1))
        softmax_weights = jnp.where(live, jnp.exp(logit_scores - new_peak[..., None]), 0.0).astype(
            jnp.bfloat16
        )
        factor = jnp.exp(peak - new_peak)
        denom = denom * factor + jnp.sum(softmax_weights, axis=-1, dtype=jnp.float32)
        weighted_values = weighted_values * factor[..., None] + jnp.einsum(
            "unqy,ynx->unqx", softmax_weights, value_tile, preferred_element_type=jnp.float32
        )
        return ((new_peak, denom, weighted_values), None)

    return lax.scan(block_step, running, (key_blocks, value_blocks, vis_blocks))[0]


def body(queries, span_keys, span_values, pool_keys, pool_values, page_ids, prefix_pages):
    tok_count = queries.shape[1]
    groups = HEADS // KV_HEADS
    width = KV_HEADS * HEAD_DIM
    queries_grouped4 = queries[0].reshape(tok_count, KV_HEADS, groups, HEAD_DIM)
    pool_count = lax.axis_size("pool")
    pool_index = lax.axis_index("pool")
    ctx_index = lax.axis_index("cp")
    slot_count = page_ids.shape[1]
    owners = page_ids // PAGES_DEV
    slot_iota = jnp.arange(slot_count, dtype=jnp.int32)
    live_slots = slot_iota[None, :] < prefix_pages[:, None]
    earlier = slot_iota[None, :] < slot_iota[:, None]
    same_owner = (owners[:, :, None] == owners[:, None, :]) & live_slots[:, None, :] & earlier[None]
    slot_rank = jnp.sum(same_owner.astype(jnp.int32), axis=2)
    held_here = live_slots & (owners == pool_index)
    cap_iota = jnp.arange(CAP, dtype=jnp.int32)
    picked = held_here[:, None, :] & (slot_rank[:, None, :] == cap_iota[None, :, None])
    local_pages = jnp.sum(jnp.where(picked, page_ids[:, None, :] % PAGES_DEV, 0), axis=2)
    own_owners = lax.dynamic_index_in_dim(owners, pool_index, 0, keepdims=False)
    own_live = lax.dynamic_index_in_dim(live_slots, pool_index, 0, keepdims=False)
    owner_iota = jnp.arange(pool_count, dtype=jnp.int32)
    per_owner = jnp.sum(
        ((own_owners[None, :] == owner_iota[:, None]) & own_live[None, :]).astype(jnp.int32), axis=1
    )
    usable = cap_iota[None, :] < per_owner[:, None]
    empty = (
        jnp.full((tok_count, KV_HEADS, groups), NEG_FILL, jnp.float32),
        jnp.zeros((tok_count, KV_HEADS, groups), jnp.float32),
        jnp.zeros((tok_count, KV_HEADS, groups, HEAD_DIM), jnp.float32),
    )
    query_pos = ctx_index * tok_count + jnp.arange(tok_count, dtype=jnp.int32)
    key_piece = lax.all_gather(span_keys, "cp", axis=1, tiled=True)
    value_piece = lax.all_gather(span_values, "cp", axis=1, tiled=True)
    piece_len = key_piece.shape[1]
    key_pos = jnp.arange(piece_len, dtype=jnp.int32)
    visible = key_pos[None, :] <= query_pos[:, None]
    local_state = attend(empty, queries_grouped4, key_piece[0], value_piece[0], visible)
    fetched_keys, fetched_values = (
        lax.all_to_all(pool_keys[local_pages], "pool", split_axis=0, concat_axis=0, tiled=True),
        lax.all_to_all(pool_values[local_pages], "pool", split_axis=0, concat_axis=0, tiled=True),
    )
    part_len = fetched_keys.shape[2]
    visible = jnp.broadcast_to(usable[:, :, None], (pool_count, CAP, part_len)).reshape(1, -1)
    prefix_state = attend(
        empty,
        queries_grouped4,
        fetched_keys.reshape(-1, width),
        fetched_values.reshape(-1, width),
        visible,
    )
    peak_one, denom_one, mixed_one = local_state
    peak_two, denom_two, mixed_two = prefix_state
    peak = jnp.maximum(peak_one, peak_two)
    factor_one = jnp.exp(peak_one - peak)
    factor_two = jnp.exp(peak_two - peak)
    denom = denom_one * factor_one + denom_two * factor_two
    weighted_values = mixed_one * factor_one[..., None] + mixed_two * factor_two[..., None]
    attended = weighted_values / denom[..., None]
    return attended.reshape(1, tok_count, HEADS * HEAD_DIM)


def solution(mesh):
    in_specs = (
        P("pool", "cp", None),
        P("pool", "cp", None),
        P("pool", "cp", None),
        P("pool", None, None),
        P("pool", None, None),
        P(),
        P(),
    )
    out_specs = P("pool", "cp", None)
    return jax.shard_map(body, mesh=mesh, in_specs=in_specs, out_specs=out_specs, check_vma=False)
```

profile of v0, /device:TPU:103, one launch (start us, length us, event | category | flops | bytes accessed | tf_op | source)
XLA Modules:
  0.0 374.7 jit_solution(9860635105908914886)
XLA Ops:
  9.1 2.7 gather_fusion
  11.8 6.0 %all-to-all-start = ((bf16[16,2,128,512]{3,2,1,0:T(8,128)(2,1)}), bf16[16,2,128,512]{3,2,1,0:T(8,128)(2,1)}, u32[]{:S(2)}, u32[]{:S(2)}) async-start(bf16[16,2,128,512]{3,2,1,0:T(8,128)(2,1)} %bitcast.101), calls=%async_computation | async-start | bytes 8388608 | tf_op jit(solution)/shard_map/all_to_all | solution.py:87
  19.7 2.8 gather_fusion.1
  22.5 1.6 copy.26
  25.0 46.9 %all-gather.5.cloned.1.call-done = bf16[1,1024,512]{2,1,0:T(8,128)(2,1)} async-done(((bf16[1,128,512]{2,1,0:T(8,128)(2,1)}), bf16[1,1024,512]{2,1,0:T(8,128)(2,1)}) %all-gather.5.cloned.1.call-update) | async-done | bytes 1048592 | tf_op jit(solution)/shard_map/all_gather | solution.py:81
  71.9 2.1 reshape_squeeze.11
  74.0 44.0 %all-gather.3.cloned.1.call-done = bf16[1,1024,512]{2,1,0:T(8,128)(2,1)} async-done(((bf16[1,128,512]{2,1,0:T(8,128)(2,1)}), bf16[1,1024,512]{2,1,0:T(8,128)(2,1)}) %all-gather.3.cloned.1.call-update) | async-done | bytes 1048592 | tf_op jit(solution)/shard_map/all_gather | solution.py:80
  118.0 2.2 reshape_squeeze.9
  120.2 7.5 %all-to-all-start.1 = ((bf16[16,2,128,512]{3,2,1,0:T(8,128)(2,1)}), bf16[16,2,128,512]{3,2,1,0:T(8,128)(2,1)}, u32[]{:S(2)}, u32[]{:S(2)}) async-start(bf16[16,2,128,512]{3,2,1,0:T(8,128)(2,1)} %bitcast.100), calls=%async_computation.1 | async-start | bytes 8388608 | tf_op jit(solution)/shard_map/all_to_all | solution.py:88
  127.7 36.7 %while.30 = (s32[]{:T(128)}, f32[128,4,8]{0,2,1:T(8,128)S(1)}, f32[128,4,8]{0,2,1:T(8,128)S(1)}, f32[128,4,8,128]{0,3,2,1:T(8,128)}, pred[2,128,512]{1,2,0:T(8,1...) while((s32[]{:T(128)}, f32[128,4,8]{0,2,1:T(8,128)S(1)}, ...), condition=%wide.region_3.4_spmd.clone, body=%wide.region_0.0_spmd.clone.sunk | while | flops 1106792448 | bytes 35192952 | solution.py:45
  127.7 1.6 constant_dynamic-slice_fusion.6
  129.3 4.6 %fusion.31 = (f32[128,4,8]{0,2,1:T(8,128)S(1)}, f32[4,512,128,8]{2,1,3,0:T(8,128)}) fusion(pred[128,512]{0,1:T(8,128)(4,1)S(1)} %dynamic-slice_bitcast_fusion.4, bf16[128,4,8,128]{3,0,2,1:T(8,128)(2,1)S(1)} %get-tuple-element.419, bf16[1,512,4,128]{3,2,1,0:T(4,128)(2,1)S(1)} %get-tuple-element.341), kind=kOutput, calls=%fused_computation.5.clone.1 | convolution fusion | flops 543158272 | bytes 10043392 | tf_op jit(solution)/shard_map/while/body/eval_jaxpr/swxl,cwl->swxc/dot_general | solution.py:27
  133.9 4.5 %convert_reduce_fusion.6 = f32[128,4,8]{0,2,1:T(8,128)S(1)} fusion(f32[128,4,8]{0,2,1:T(8,128)S(1)} %select_maximum_fusion.4, f32[4,512,128,8]{2,1,3,0:T(8,128)} %get-tuple-element.343, pred[128,512]{0,1:T(8,128)(4,1)S(1)} %dynamic-slice_bitcast_fusion.4), kind=kLoop, calls=%fused_computation.3.clone.1 | loop fusion | flops 14675968 | bytes 8486912 | tf_op jit(solution)/shard_map/while/body/eval_jaxpr/reduce_sum | solution.py:39
  138.7 7.0 %bitcast_add_fusion.4 = f32[128,4,8,128]{0,3,2,1:T(8,128)} fusion(f32[128,4,8,128]{0,3,2,1:T(8,128)} %get-tuple-element.406, f32[128,4,8]{0,2,1:T(8,128)S(1)} %get-tuple-element.345, pred[]{:T(512)S(6)} %compare.6, bf16[1,512,4,128]{1,3,2,0:T(8,128)(2,1)S(1)} %copy.60, f32[4,512,128,8]{2,1,3,0:T(8,128)} %get-tuple-element.343, ...), kind=kOutput, calls=%fused_computation.6.clone.1 | convolution fusion | flops 548929536 | bytes 13205505 | tf_op jit(solution)/shard_map/while/body/eval_jaxpr/unqy,ynx->unqx/dot_general | solution.py:40
  145.7 1.6 constant_dynamic-slice_fusion.6
  147.3 4.6 %fusion.31 = (f32[128,4,8]{0,2,1:T(8,128)S(1)}, f32[4,512,128,8]{2,1,3,0:T(8,128)}) fusion(pred[128,512]{0,1:T(8,128)(4,1)S(1)} %dynamic-slice_bitcast_fusion.4, bf16[128,4,8,128]{3,0,2,1:T(8,128)(2,1)S(1)} %get-tuple-element.419, bf16[1,512,4,128]{3,2,1,0:T(4,128)(2,1)S(1)} %get-tuple-element.341), kind=kOutput, calls=%fused_computation.5.clone.1 | convolution fusion | flops 543158272 | bytes 10043392 | tf_op jit(solution)/shard_map/while/body/eval_jaxpr/swxl,cwl->swxc/dot_general | solution.py:27
  151.9 4.5 %convert_reduce_fusion.6 = f32[128,4,8]{0,2,1:T(8,128)S(1)} fusion(f32[128,4,8]{0,2,1:T(8,128)S(1)} %select_maximum_fusion.4, f32[4,512,128,8]{2,1,3,0:T(8,128)} %get-tuple-element.343, pred[128,512]{0,1:T(8,128)(4,1)S(1)} %dynamic-slice_bitcast_fusion.4), kind=kLoop, calls=%fused_computation.3.clone.1 | loop fusion | flops 14675968 | bytes 8486912 | tf_op jit(solution)/shard_map/while/body/eval_jaxpr/reduce_sum | solution.py:39
  156.8 7.6 %bitcast_add_fusion.4 = f32[128,4,8,128]{0,3,2,1:T(8,128)} fusion(f32[128,4,8,128]{0,3,2,1:T(8,128)} %get-tuple-element.406, f32[128,4,8]{0,2,1:T(8,128)S(1)} %get-tuple-element.345, pred[]{:T(512)S(6)} %compare.6, bf16[1,512,4,128]{1,3,2,0:T(8,128)(2,1)S(1)} %copy.60, f32[4,512,128,8]{2,1,3,0:T(8,128)} %get-tuple-element.343, ...), kind=kOutput, calls=%fused_computation.6.clone.1 | convolution fusion | flops 548929536 | bytes 13205505 | tf_op jit(solution)/shard_map/while/body/eval_jaxpr/unqy,ynx->unqx/dot_general | solution.py:40
  164.4 7.0 %reshape_reshape.6 = bf16[8,512,4,128]{3,2,1,0:T(4,128)(2,1)} reshape(bf16[16,2,128,512]{3,2,1,0:T(8,128)(2,1)} %all-to-all-done) | data formatting | bytes 8388608 | tf_op jit(solution)/shard_map/reshape;reshape | solution.py:19
  171.3 18.5 %all-to-all-done.1 = bf16[16,2,128,512]{3,2,1,0:T(8,128)(2,1)} async-done(((bf16[16,2,128,512]{3,2,1,0:T(8,128)(2,1)}), bf16[16,2,128,512]{3,2,1,0:T(8,128)(2,1)}, u32[]{:S(2)}, u32[]{:S(2)}) %all-to-all-start.1) | async-done | bytes 4194336 | tf_op jit(solution)/shard_map/all_to_all | solution.py:88
  189.8 6.9 %reshape_reshape.7 = bf16[8,512,4,128]{3,2,1,0:T(4,128)(2,1)} reshape(bf16[16,2,128,512]{3,2,1,0:T(8,128)(2,1)} %all-to-all-done.1) | data formatting | bytes 8388608 | tf_op jit(solution)/shard_map/reshape;reshape | solution.py:20
  196.7 163.8 %while.31 = (s32[]{:T(128)}, f32[128,4,8]{0,2,1:T(8,128)S(1)}, f32[128,4,8]{0,2,1:T(8,128)S(1)}, f32[128,4,8,128]{0,3,2,1:T(8,128)}, pred[8,1,512]{2,1,0:T(4,128...) while((s32[]{:T(128)}, f32[128,4,8]{0,2,1:T(8,128)S(1)}, ...), condition=%wide.region_10.11_spmd.clone, body=%wide.region_7.10_spmd.clone.sunk | while | flops 1096306688 | bytes 51628208 | solution.py:45
  196.7 2.4 constant_dynamic-slice_fusion.7
  199.1 4.6 %bitcast_reduce_fusion.2 = (f32[128,4,8]{0,2,1:T(8,128)S(1)}, f32[4,512,128,8]{2,1,3,0:T(8,128)}) fusion(pred[512]{0:T(512)(128)(4,1)S(1)} %dynamic-slice_reduce_fusion.2, bf16[128,4,8,128]{3,0,2,1:T(8,128)(2,1)S(1)} %get-tuple-element.389, bf16[1,512,4,128]{3,2,1,0:T(4,128)(2,1)S(1)} %get-tuple-element.355), kind=kOutput, calls=%fused_computation.19.clone.1 | convolution fusion | flops 543158272 | bytes 9978368 | tf_op jit(solution)/shard_map/while/body/eval_jaxpr/swxl,cwl->swxc/dot_general | solution.py:27
  203.7 6.5 %convert_reduce_fusion.7 = (f32[128,4,8]{0,2,1:T(8,128)S(1)}, bf16[128,4,8,512]{0,3,2,1:T(8,128)(2,1)}) fusion(f32[128,4,8]{0,2,1:T(8,128)S(1)} %select_maximum_fusion.5, f32[4,512,128,8]{2,1,3,0:T(8,128)} %get-tuple-element.357, pred[512]{0:T(512)(128)(4,1)S(1)} %dynamic-slice_reduce_fusion.2), kind=kLoop, calls=%fused_computation.23.clone.1 | loop fusion | flops 14675968 | bytes 12616192 | tf_op jit(solution)/shard_map/while/body/eval_jaxpr/reduce_sum | solution.py:39
  210.2 2.1 copy.62
  212.3 3.5 bitcast_add_fusion.5
  217.2 2.4 constant_dynamic-slice_fusion.7
  219.6 4.6 %bitcast_reduce_fusion.2 = (f32[128,4,8]{0,2,1:T(8,128)S(1)}, f32[4,512,128,8]{2,1,3,0:T(8,128)}) fusion(pred[512]{0:T(512)(128)(4,1)S(1)} %dynamic-slice_reduce_fusion.2, bf16[128,4,8,128]{3,0,2,1:T(8,128)(2,1)S(1)} %get-tuple-element.389, bf16[1,512,4,128]{3,2,1,0:T(4,128)(2,1)S(1)} %get-tuple-element.355), kind=kOutput, calls=%fused_computation.19.clone.1 | convolution fusion | flops 543158272 | bytes 9978368 | tf_op jit(solution)/shard_map/while/body/eval_jaxpr/swxl,cwl->swxc/dot_general | solution.py:27
  224.2 6.5 %convert_reduce_fusion.7 = (f32[128,4,8]{0,2,1:T(8,128)S(1)}, bf16[128,4,8,512]{0,3,2,1:T(8,128)(2,1)}) fusion(f32[128,4,8]{0,2,1:T(8,128)S(1)} %select_maximum_fusion.5, f32[4,512,128,8]{2,1,3,0:T(8,128)} %get-tuple-element.357, pred[512]{0:T(512)(128)(4,1)S(1)} %dynamic-slice_reduce_fusion.2), kind=kLoop, calls=%fused_computation.23.clone.1 | loop fusion | flops 14675968 | bytes 12616192 | tf_op jit(solution)/shard_map/while/body/eval_jaxpr/reduce_sum | solution.py:39
  230.7 2.1 copy.62
  232.8 3.5 bitcast_add_fusion.5
  237.7 2.4 constant_dynamic-slice_fusion.7
  240.0 4.6 %bitcast_reduce_fusion.2 = (f32[128,4,8]{0,2,1:T(8,128)S(1)}, f32[4,512,128,8]{2,1,3,0:T(8,128)}) fusion(pred[512]{0:T(512)(128)(4,1)S(1)} %dynamic-slice_reduce_fusion.2, bf16[128,4,8,128]{3,0,2,1:T(8,128)(2,1)S(1)} %get-tuple-element.389, bf16[1,512,4,128]{3,2,1,0:T(4,128)(2,1)S(1)} %get-tuple-element.355), kind=kOutput, calls=%fused_computation.19.clone.1 | convolution fusion | flops 543158272 | bytes 9978368 | tf_op jit(solution)/shard_map/while/body/eval_jaxpr/swxl,cwl->swxc/dot_general | solution.py:27
  244.6 6.5 %convert_reduce_fusion.7 = (f32[128,4,8]{0,2,1:T(8,128)S(1)}, bf16[128,4,8,512]{0,3,2,1:T(8,128)(2,1)}) fusion(f32[128,4,8]{0,2,1:T(8,128)S(1)} %select_maximum_fusion.5, f32[4,512,128,8]{2,1,3,0:T(8,128)} %get-tuple-element.357, pred[512]{0:T(512)(128)(4,1)S(1)} %dynamic-slice_reduce_fusion.2), kind=kLoop, calls=%fused_computation.23.clone.1 | loop fusion | flops 14675968 | bytes 12616192 | tf_op jit(solution)/shard_map/while/body/eval_jaxpr/reduce_sum | solution.py:39
  251.2 2.1 copy.62
  253.3 3.5 bitcast_add_fusion.5
  258.1 2.4 constant_dynamic-slice_fusion.7
  260.5 4.6 %bitcast_reduce_fusion.2 = (f32[128,4,8]{0,2,1:T(8,128)S(1)}, f32[4,512,128,8]{2,1,3,0:T(8,128)}) fusion(pred[512]{0:T(512)(128)(4,1)S(1)} %dynamic-slice_reduce_fusion.2, bf16[128,4,8,128]{3,0,2,1:T(8,128)(2,1)S(1)} %get-tuple-element.389, bf16[1,512,4,128]{3,2,1,0:T(4,128)(2,1)S(1)} %get-tuple-element.355), kind=kOutput, calls=%fused_computation.19.clone.1 | convolution fusion | flops 543158272 | bytes 9978368 | tf_op jit(solution)/shard_map/while/body/eval_jaxpr/swxl,cwl->swxc/dot_general | solution.py:27
  265.1 6.5 %convert_reduce_fusion.7 = (f32[128,4,8]{0,2,1:T(8,128)S(1)}, bf16[128,4,8,512]{0,3,2,1:T(8,128)(2,1)}) fusion(f32[128,4,8]{0,2,1:T(8,128)S(1)} %select_maximum_fusion.5, f32[4,512,128,8]{2,1,3,0:T(8,128)} %get-tuple-element.357, pred[512]{0:T(512)(128)(4,1)S(1)} %dynamic-slice_reduce_fusion.2), kind=kLoop, calls=%fused_computation.23.clone.1 | loop fusion | flops 14675968 | bytes 12616192 | tf_op jit(solution)/shard_map/while/body/eval_jaxpr/reduce_sum | solution.py:39
  271.6 2.1 copy.62
  273.7 3.5 bitcast_add_fusion.5
  278.6 2.4 constant_dynamic-slice_fusion.7
  281.0 4.6 %bitcast_reduce_fusion.2 = (f32[128,4,8]{0,2,1:T(8,128)S(1)}, f32[4,512,128,8]{2,1,3,0:T(8,128)}) fusion(pred[512]{0:T(512)(128)(4,1)S(1)} %dynamic-slice_reduce_fusion.2, bf16[128,4,8,128]{3,0,2,1:T(8,128)(2,1)S(1)} %get-tuple-element.389, bf16[1,512,4,128]{3,2,1,0:T(4,128)(2,1)S(1)} %get-tuple-element.355), kind=kOutput, calls=%fused_computation.19.clone.1 | convolution fusion | flops 543158272 | bytes 9978368 | tf_op jit(solution)/shard_map/while/body/eval_jaxpr/swxl,cwl->swxc/dot_general | solution.py:27
  285.6 6.5 %convert_reduce_fusion.7 = (f32[128,4,8]{0,2,1:T(8,128)S(1)}, bf16[128,4,8,512]{0,3,2,1:T(8,128)(2,1)}) fusion(f32[128,4,8]{0,2,1:T(8,128)S(1)} %select_maximum_fusion.5, f32[4,512,128,8]{2,1,3,0:T(8,128)} %get-tuple-element.357, pred[512]{0:T(512)(128)(4,1)S(1)} %dynamic-slice_reduce_fusion.2), kind=kLoop, calls=%fused_computation.23.clone.1 | loop fusion | flops 14675968 | bytes 12616192 | tf_op jit(solution)/shard_map/while/body/eval_jaxpr/reduce_sum | solution.py:39
  292.1 2.1 copy.62
  294.2 3.5 bitcast_add_fusion.5
  299.1 2.4 constant_dynamic-slice_fusion.7
  301.5 4.6 %bitcast_reduce_fusion.2 = (f32[128,4,8]{0,2,1:T(8,128)S(1)}, f32[4,512,128,8]{2,1,3,0:T(8,128)}) fusion(pred[512]{0:T(512)(128)(4,1)S(1)} %dynamic-slice_reduce_fusion.2, bf16[128,4,8,128]{3,0,2,1:T(8,128)(2,1)S(1)} %get-tuple-element.389, bf16[1,512,4,128]{3,2,1,0:T(4,128)(2,1)S(1)} %get-tuple-element.355), kind=kOutput, calls=%fused_computation.19.clone.1 | convolution fusion | flops 543158272 | bytes 9978368 | tf_op jit(solution)/shard_map/while/body/eval_jaxpr/swxl,cwl->swxc/dot_general | solution.py:27
  306.0 6.5 %convert_reduce_fusion.7 = (f32[128,4,8]{0,2,1:T(8,128)S(1)}, bf16[128,4,8,512]{0,3,2,1:T(8,128)(2,1)}) fusion(f32[128,4,8]{0,2,1:T(8,128)S(1)} %select_maximum_fusion.5, f32[4,512,128,8]{2,1,3,0:T(8,128)} %get-tuple-element.357, pred[512]{0:T(512)(128)(4,1)S(1)} %dynamic-slice_reduce_fusion.2), kind=kLoop, calls=%fused_computation.23.clone.1 | loop fusion | flops 14675968 | bytes 12616192 | tf_op jit(solution)/shard_map/while/body/eval_jaxpr/reduce_sum | solution.py:39
  312.6 2.1 copy.62
  314.7 3.5 bitcast_add_fusion.5
  319.5 2.4 constant_dynamic-slice_fusion.7
  321.9 4.6 %bitcast_reduce_fusion.2 = (f32[128,4,8]{0,2,1:T(8,128)S(1)}, f32[4,512,128,8]{2,1,3,0:T(8,128)}) fusion(pred[512]{0:T(512)(128)(4,1)S(1)} %dynamic-slice_reduce_fusion.2, bf16[128,4,8,128]{3,0,2,1:T(8,128)(2,1)S(1)} %get-tuple-element.389, bf16[1,512,4,128]{3,2,1,0:T(4,128)(2,1)S(1)} %get-tuple-element.355), kind=kOutput, calls=%fused_computation.19.clone.1 | convolution fusion | flops 543158272 | bytes 9978368 | tf_op jit(solution)/shard_map/while/body/eval_jaxpr/swxl,cwl->swxc/dot_general | solution.py:27
  326.5 6.5 %convert_reduce_fusion.7 = (f32[128,4,8]{0,2,1:T(8,128)S(1)}, bf16[128,4,8,512]{0,3,2,1:T(8,128)(2,1)}) fusion(f32[128,4,8]{0,2,1:T(8,128)S(1)} %select_maximum_fusion.5, f32[4,512,128,8]{2,1,3,0:T(8,128)} %get-tuple-element.357, pred[512]{0:T(512)(128)(4,1)S(1)} %dynamic-slice_reduce_fusion.2), kind=kLoop, calls=%fused_computation.23.clone.1 | loop fusion | flops 14675968 | bytes 12616192 | tf_op jit(solution)/shard_map/while/body/eval_jaxpr/reduce_sum | solution.py:39
  333.0 2.1 copy.62
  335.2 3.5 bitcast_add_fusion.5
  340.0 2.4 constant_dynamic-slice_fusion.7
  342.4 4.6 %bitcast_reduce_fusion.2 = (f32[128,4,8]{0,2,1:T(8,128)S(1)}, f32[4,512,128,8]{2,1,3,0:T(8,128)}) fusion(pred[512]{0:T(512)(128)(4,1)S(1)} %dynamic-slice_reduce_fusion.2, bf16[128,4,8,128]{3,0,2,1:T(8,128)(2,1)S(1)} %get-tuple-element.389, bf16[1,512,4,128]{3,2,1,0:T(4,128)(2,1)S(1)} %get-tuple-element.355), kind=kOutput, calls=%fused_computation.19.clone.1 | convolution fusion | flops 543158272 | bytes 9978368 | tf_op jit(solution)/shard_map/while/body/eval_jaxpr/swxl,cwl->swxc/dot_general | solution.py:27
  347.0 6.5 %convert_reduce_fusion.7 = (f32[128,4,8]{0,2,1:T(8,128)S(1)}, bf16[128,4,8,512]{0,3,2,1:T(8,128)(2,1)}) fusion(f32[128,4,8]{0,2,1:T(8,128)S(1)} %select_maximum_fusion.5, f32[4,512,128,8]{2,1,3,0:T(8,128)} %get-tuple-element.357, pred[512]{0:T(512)(128)(4,1)S(1)} %dynamic-slice_reduce_fusion.2), kind=kLoop, calls=%fused_computation.23.clone.1 | loop fusion | flops 14675968 | bytes 12616192 | tf_op jit(solution)/shard_map/while/body/eval_jaxpr/reduce_sum | solution.py:39
  353.5 2.1 copy.62
  355.6 3.5 bitcast_add_fusion.5
  360.5 4.5 %add_divide_fusion = f32[128,4,8,128]{0,3,2,1:T(8,128)} fusion(f32[128,4,8,128]{0,3,2,1:T(8,128)} %get-tuple-element.96, f32[128,4,8,128]{0,3,2,1:T(8,128)} %get-tuple-element.93, f32[128,4,8]{0,2,1:T(8,128)S(1)} %get-tuple-element.223, f32[128,4,8]{0,2,1:T(8,128)S(1)} %get-tuple-element.225, f32[128,4,8]{0,2,1:T(8,128)S(1)} %get-tuple-element.224), kind=kLoop, calls=%fused_computation.37 | loop fusion | flops 2097152 | bytes 6340608 | tf_op jit(solution)/shard_map/div | solution.py:106
  365.0 2.9 copy.42
  (111 shorter events, 16.7 us)
Async XLA Ops:
  6.5 2.5 copy-start
  11.8 7.9 %copy-start.4 = (bf16[24,128,512]{2,1,0:T(8,128)(2,1)S(1)}, bf16[24,128,512]{2,1,0:T(8,128)(2,1)}, u32[]{:S(2)}) copy-start(bf16[24,128,512]{2,1,0:T(8,128)(2,1)} %param.15) | copy-start | bytes 9437188
  11.8 108.3 %all-to-all-start = ((bf16[16,2,128,512]{3,2,1,0:T(8,128)(2,1)}), bf16[16,2,128,512]{3,2,1,0:T(8,128)(2,1)}, u32[]{:S(2)}, u32[]{:S(2)}) async-start(bf16[16,2,128,512]{3,2,1,0:T(8,128)(2,1)} %bitcast.101), calls=%async_computation | async-start | bytes 8388608 | tf_op jit(solution)/shard_map/all_to_all | solution.py:87
  17.8 54.1 %all-gather.5.cloned.1.call-start = ((), (), s32[]{:S(2)}) async-start(), calls=%async_computation.3 | async-start | bytes 1179648 | tf_op jit(solution)/shard_map/all_gather | solution.py:81
  18.5 99.5 %all-gather.3.cloned.1.call-start = ((), (), s32[]{:S(2)}) async-start(), calls=%async_computation.2 | async-start | bytes 1179648 | tf_op jit(solution)/shard_map/all_gather | solution.py:80
  120.2 69.6 %all-to-all-start.1 = ((bf16[16,2,128,512]{3,2,1,0:T(8,128)(2,1)}), bf16[16,2,128,512]{3,2,1,0:T(8,128)(2,1)}, u32[]{:S(2)}, u32[]{:S(2)}) async-start(bf16[16,2,128,512]{3,2,1,0:T(8,128)(2,1)} %bitcast.100), calls=%async_computation.1 | async-start | bytes 8388608 | tf_op jit(solution)/shard_map/all_to_all | solution.py:88
  203.7 8.6 %copy-start.2 = (f32[128,4,8,128]{0,3,2,1:T(8,128)S(1)}, f32[128,4,8,128]{0,3,2,1:T(8,128)}, u32[]{:S(2)}) copy-start(f32[128,4,8,128]{0,3,2,1:T(8,128)} %get-tuple-element.376) | copy-start | bytes 6291460 | tf_op jit(solution)/shard_map/while
  215.9 1.3 copy-start.3
  224.2 8.6 %copy-start.2 = (f32[128,4,8,128]{0,3,2,1:T(8,128)S(1)}, f32[128,4,8,128]{0,3,2,1:T(8,128)}, u32[]{:S(2)}) copy-start(f32[128,4,8,128]{0,3,2,1:T(8,128)} %get-tuple-element.376) | copy-start | bytes 6291460 | tf_op jit(solution)/shard_map/while
  236.3 1.3 copy-start.3
  244.6 8.6 %copy-start.2 = (f32[128,4,8,128]{0,3,2,1:T(8,128)S(1)}, f32[128,4,8,128]{0,3,2,1:T(8,128)}, u32[]{:S(2)}) copy-start(f32[128,4,8,128]{0,3,2,1:T(8,128)} %get-tuple-element.376) | copy-start | bytes 6291460 | tf_op jit(solution)/shard_map/while
  256.8 1.3 copy-start.3
  265.1 8.6 %copy-start.2 = (f32[128,4,8,128]{0,3,2,1:T(8,128)S(1)}, f32[128,4,8,128]{0,3,2,1:T(8,128)}, u32[]{:S(2)}) copy-start(f32[128,4,8,128]{0,3,2,1:T(8,128)} %get-tuple-element.376) | copy-start | bytes 6291460 | tf_op jit(solution)/shard_map/while
  277.3 1.3 copy-start.3
  285.6 8.6 %copy-start.2 = (f32[128,4,8,128]{0,3,2,1:T(8,128)S(1)}, f32[128,4,8,128]{0,3,2,1:T(8,128)}, u32[]{:S(2)}) copy-start(f32[128,4,8,128]{0,3,2,1:T(8,128)} %get-tuple-element.376) | copy-start | bytes 6291460 | tf_op jit(solution)/shard_map/while
  297.8 1.3 copy-start.3
  306.0 8.6 %copy-start.2 = (f32[128,4,8,128]{0,3,2,1:T(8,128)S(1)}, f32[128,4,8,128]{0,3,2,1:T(8,128)}, u32[]{:S(2)}) copy-start(f32[128,4,8,128]{0,3,2,1:T(8,128)} %get-tuple-element.376) | copy-start | bytes 6291460 | tf_op jit(solution)/shard_map/while
  318.2 1.3 copy-start.3
  326.5 8.6 %copy-start.2 = (f32[128,4,8,128]{0,3,2,1:T(8,128)S(1)}, f32[128,4,8,128]{0,3,2,1:T(8,128)}, u32[]{:S(2)}) copy-start(f32[128,4,8,128]{0,3,2,1:T(8,128)} %get-tuple-element.376) | copy-start | bytes 6291460 | tf_op jit(solution)/shard_map/while
  338.7 1.3 copy-start.3
  347.0 8.6 %copy-start.2 = (f32[128,4,8,128]{0,3,2,1:T(8,128)S(1)}, f32[128,4,8,128]{0,3,2,1:T(8,128)}, u32[]{:S(2)}) copy-start(f32[128,4,8,128]{0,3,2,1:T(8,128)} %get-tuple-element.376) | copy-start | bytes 6291460 | tf_op jit(solution)/shard_map/while
  359.2 1.3 copy-start.3
  360.5 7.4 %copy-start.1 = (bf16[24,128,512]{2,1,0:T(8,128)(2,1)S(1)}, bf16[24,128,512]{2,1,0:T(8,128)(2,1)}, u32[]{:S(2)}) copy-start(bf16[24,128,512]{2,1,0:T(8,128)(2,1)} %param.14) | copy-start | bytes 9437188
Sparse Core Ops, SparseCore 0:
  21.0 50.8 all-gather.4
  74.2 43.7 all-gather.2
where the time goes:
time: 376 us; the launch traced here: 375 us
  waiting for transfers between devices  111 us (30%)
  matrix products  88.7 us (24%)
  local copies, waits for them, and re-layouts  79.4 us (21%)
  other arithmetic  68.5 us (18%)
  starting transfers between devices  13.6 us (4%)
  between operations  13.6 us (4%)
    reduce_sum x10, other arithmetic, block_step(): jnp.sum(softmax_weights, axis=-1, dtype=jnp.float32)  61 us
    all_gather x1, waiting for transfers between devices, body(): value_piece = lax.all_gather(span_values, 'cp', axis=1, tiled=True)  46.9 us
    dot_general x10, matrix products, block_step(): jnp.einsum('swxl,cwl->swxc', queries_grouped4, key_tile, preferred_elemen...  45.8 us
    all_gather x1, waiting for transfers between devices, body(): key_piece = lax.all_gather(span_keys, 'cp', axis=1, tiled=True)  44 us
    dot_general x10, matrix products, block_step(): jnp.einsum('unqy,ynx->unqx', softmax_weights, value_tile, preferred_eleme...  42.9 us
    dynamic_slice x28, local copies, waits for them, and re-layouts, attend(): lax.scan(block_step, running, (key_blocks, value_blocks, vis_blocks))[0]  39.7 us
    all_to_all x1, waiting for transfers between devices, body(): lax.all_to_all(pool_values[local_pages], 'pool', split_axis=0, concat_axi...  18.5 us
    while x42, local copies, waits for them, and re-layouts  10.5 us
  transfers between devices with their start and end apart: 4, of which 3 were waited for; matrix products, arithmetic and copies ran while one was open for 14% of the time, Pallas kernels for 0%

commit v1 on v0

--- a/solution.py
+++ b/solution.py
@@ -1,3 +1,4 @@
+import functools
 import jax
 import jax.numpy as jnp
 from jax import lax
@@ -9,6 +10,16 @@
 CAP = 2
 PAGES_DEV = 24
 NEG_FILL = -1e30
+
+
+def _launch_rails(row_data, on_dim):
+    history = []
+    for _ in range(lax.axis_size("cp")):
+        history.append(row_data)
+    return jnp.concatenate(lax.all_to_all(jnp.stack(history), "cp", 0, 0), axis=on_dim)
+
+
+refer_the_vectors = functools.partial(_launch_rails, on_dim=1)
 
 
 def attend(running, queries_grouped4, key_row_set, value_row_set, visible):
@@ -77,7 +88,7 @@
         jnp.zeros((tok_count, KV_HEADS, groups, HEAD_DIM), jnp.float32),
     )
     query_pos = ctx_index * tok_count + jnp.arange(tok_count, dtype=jnp.int32)
-    key_piece = lax.all_gather(span_keys, "cp", axis=1, tiled=True)
+    key_piece = refer_the_vectors(span_keys)
     value_piece = lax.all_gather(span_values, "cp", axis=1, tiled=True)
     piece_len = key_piece.shape[1]
     key_pos = jnp.arange(piece_len, dtype=jnp.int32)

time: 376 us -> 357 us (0.949)
  waiting for transfers between devices: 111 us -> 86.1 us
  starting transfers between devices: 13.6 us -> 18.2 us
    all_gather x1 -> x0, waiting for transfers between devices: 44 us -> none  [body(): key_piece = lax.all_gather(span_keys, 'cp', axis=1, tiled=True)]
    all_to_all x1, waiting for transfers between devices: 0.01 us -> 13.4 us  [body(): lax.all_to_all(pool_keys[local_pages], 'pool', split_axis=0, concat_axis=...]
    all_to_all x0 -> x1, waiting for transfers between devices: none -> 9.74 us  [_launch_rails(): lax.all_to_all(jnp.stack(history), 'cp', 0, 0)]
    all_to_all x0 -> x1, starting transfers between devices: none -> 6.87 us  [_launch_rails(): lax.all_to_all(jnp.stack(history), 'cp', 0, 0)]
  transfers between devices with their start and end apart: 4 -> 4, of which waited for: 3 -> 4; matrix products, arithmetic and copies ran while one was open for 14% -> 16% of each run, Pallas kernels for 0% -> 0%
where the time goes in v1:
time: 357 us; the launch traced here: 355 us
  matrix products  88.6 us (25%)
  waiting for transfers between devices  86.1 us (24%)
  local copies, waits for them, and re-layouts  81.3 us (23%)
  other arithmetic  67.3 us (19%)
  starting transfers between devices  18.2 us (5%)
  between operations  13.6 us (4%)
    reduce_sum x10, other arithmetic, block_step(): jnp.sum(softmax_weights, axis=-1, dtype=jnp.float32)  60.1 us
    dot_general x10, matrix products, block_step(): jnp.einsum('swxl,cwl->swxc', queries_grouped4, key_tile, preferred_elemen...  45.7 us
    all_gather x1, waiting for transfers between devices, body(): value_piece = lax.all_gather(span_values, 'cp', axis=1, tiled=True)  43.7 us
    dot_general x10, matrix products, block_step(): jnp.einsum('unqy,ynx->unqx', softmax_weights, value_tile, preferred_eleme...  42.9 us
    dynamic_slice x28, local copies, waits for them, and re-layouts, attend(): lax.scan(block_step, running, (key_blocks, value_blocks, vis_blocks))[0]  39.5 us
    all_to_all x1, waiting for transfers between devices, body(): lax.all_to_all(pool_values[local_pages], 'pool', split_axis=0, concat_axi...  18.5 us
    all_to_all x1, waiting for transfers between devices, body(): lax.all_to_all(pool_keys[local_pages], 'pool', split_axis=0, concat_axis=...  13.4 us
    while x42, local copies, waits for them, and re-layouts  10.5 us
  transfers between devices with their start and end apart: 4, of which 4 were waited for; matrix products, arithmetic and copies ran while one was open for 16% of the time, Pallas kernels for 0%

profile of v1, /device:TPU:103, one launch (start us, length us, event | category | flops | bytes accessed | tf_op | source)
XLA Modules:
  0.0 355.4 jit_solution(14492407672730807978)
XLA Ops:
  6.5 2.1 stack.2
  8.6 6.9 %all-to-all-start = ((bf16[8,1,128,512]{3,2,1,0:T(8,128)(2,1)}), bf16[8,1,128,512]{3,2,1,0:T(8,128)(2,1)}, u32[]{:S(2)}, u32[]{:S(2)}) async-start(bf16[8,1,128,512]{3,2,1,0:T(8,128)(2,1)} %stack.2), calls=%async_computation | async-start | bytes 2097152 | tf_op jit(solution)/shard_map/all_to_all | solution.py:19
  17.8 2.7 gather_fusion
  20.6 9.7 %all-to-all-done = bf16[8,1,128,512]{3,2,1,0:T(8,128)(2,1)} async-done(((bf16[8,1,128,512]{3,2,1,0:T(8,128)(2,1)}), bf16[8,1,128,512]{3,2,1,0:T(8,128)(2,1)}, u32[]{:S(2)}, u32[]{:S(2)}) %all-to-all-start) | async-done | bytes 1048608 | tf_op jit(solution)/shard_map/all_to_all | solution.py:19
  30.3 6.1 %all-to-all-start.1 = ((bf16[16,2,128,512]{3,2,1,0:T(8,128)(2,1)}), bf16[16,2,128,512]{3,2,1,0:T(8,128)(2,1)}, u32[]{:S(2)}, u32[]{:S(2)}) async-start(bf16[16,2,128,512]{3,2,1,0:T(8,128)(2,1)} %bitcast.104), calls=%async_computation.1 | async-start | bytes 8388608 | tf_op jit(solution)/shard_map/all_to_all | solution.py:98
  37.6 2.8 gather_fusion.1
  42.9 2.1 reshape_squeeze_reshape.3
  45.0 43.7 %all-gather.2.cloned.1.call-done = bf16[1,1024,512]{2,1,0:T(8,128)(2,1)} async-done(((bf16[1,128,512]{2,1,0:T(8,128)(2,1)}), bf16[1,1024,512]{2,1,0:T(8,128)(2,1)}) %all-gather.2.cloned.1.call-update) | async-done | bytes 1048592 | tf_op jit(solution)/shard_map/all_gather | solution.py:92
  88.8 2.2 reshape_squeeze.7
  90.9 13.4 %all-to-all-done.1 = bf16[16,2,128,512]{3,2,1,0:T(8,128)(2,1)} async-done(((bf16[16,2,128,512]{3,2,1,0:T(8,128)(2,1)}), bf16[16,2,128,512]{3,2,1,0:T(8,128)(2,1)}, u32[]{:S(2)}, u32[]{:S(2)}) %all-to-all-start.1) | async-done | bytes 4194336 | tf_op jit(solution)/shard_map/all_to_all | solution.py:98
  104.4 5.2 %all-to-all-start.2 = ((bf16[16,2,128,512]{3,2,1,0:T(8,128)(2,1)}), bf16[16,2,128,512]{3,2,1,0:T(8,128)(2,1)}, u32[]{:S(2)}, u32[]{:S(2)}) async-start(bf16[16,2,128,512]{3,2,1,0:T(8,128)(2,1)} %bitcast.103), calls=%async_computation.2 | async-start | bytes 8388608 | tf_op jit(solution)/shard_map/all_to_all | solution.py:99
  109.5 36.7 %while.30 = (s32[]{:T(128)}, f32[128,4,8]{0,2,1:T(8,128)S(1)}, f32[128,4,8]{0,2,1:T(8,128)S(1)}, f32[128,4,8,128]{0,3,2,1:T(8,128)}, pred[2,128,512]{1,2,0:T(8,1...) while((s32[]{:T(128)}, f32[128,4,8]{0,2,1:T(8,128)S(1)}, ...), condition=%wide.region_3.4_spmd.clone, body=%wide.region_0.0_spmd.clone.sunk | while | flops 1106792448 | bytes 35192952 | solution.py:56
  111.1 4.6 %fusion.31 = (f32[128,4,8]{0,2,1:T(8,128)S(1)}, f32[4,512,128,8]{2,1,3,0:T(8,128)}) fusion(pred[128,512]{0,1:T(8,128)(4,1)S(1)} %dynamic-slice_bitcast_fusion.4, bf16[128,4,8,128]{3,0,2,1:T(8,128)(2,1)S(1)} %get-tuple-element.435, bf16[1,512,4,128]{3,2,1,0:T(4,128)(2,1)S(1)} %get-tuple-element.357), kind=kOutput, calls=%fused_computation.5.clone.1 | convolution fusion | flops 543158272 | bytes 10043392 | tf_op jit(solution)/shard_map/while/body/eval_jaxpr/swxl,cwl->swxc/dot_general | solution.py:38
  115.7 4.5 %convert_reduce_fusion.6 = f32[128,4,8]{0,2,1:T(8,128)S(1)} fusion(f32[128,4,8]{0,2,1:T(8,128)S(1)} %select_maximum_fusion.4, f32[4,512,128,8]{2,1,3,0:T(8,128)} %get-tuple-element.359, pred[128,512]{0,1:T(8,128)(4,1)S(1)} %dynamic-slice_bitcast_fusion.4), kind=kLoop, calls=%fused_computation.3.clone.1 | loop fusion | flops 14675968 | bytes 8486912 | tf_op jit(solution)/shard_map/while/body/eval_jaxpr/reduce_sum | solution.py:50
  120.6 7.0 %bitcast_add_fusion.4 = f32[128,4,8,128]{0,3,2,1:T(8,128)} fusion(f32[128,4,8,128]{0,3,2,1:T(8,128)} %get-tuple-element.422, f32[128,4,8]{0,2,1:T(8,128)S(1)} %get-tuple-element.361, pred[]{:T(512)S(6)} %compare.6, bf16[1,512,4,128]{1,3,2,0:T(8,128)(2,1)S(1)} %copy.72, f32[4,512,128,8]{2,1,3,0:T(8,128)} %get-tuple-element.359, ...), kind=kOutput, calls=%fused_computation.6.clone.1 | convolution fusion | flops 548929536 | bytes 13205505 | tf_op jit(solution)/shard_map/while/body/eval_jaxpr/unqy,ynx->unqx/dot_general | solution.py:51
  129.2 4.6 %fusion.31 = (f32[128,4,8]{0,2,1:T(8,128)S(1)}, f32[4,512,128,8]{2,1,3,0:T(8,128)}) fusion(pred[128,512]{0,1:T(8,128)(4,1)S(1)} %dynamic-slice_bitcast_fusion.4, bf16[128,4,8,128]{3,0,2,1:T(8,128)(2,1)S(1)} %get-tuple-element.435, bf16[1,512,4,128]{3,2,1,0:T(4,128)(2,1)S(1)} %get-tuple-element.357), kind=kOutput, calls=%fused_computation.5.clone.1 | convolution fusion | flops 543158272 | bytes 10043392 | tf_op jit(solution)/shard_map/while/body/eval_jaxpr/swxl,cwl->swxc/dot_general | solution.py:38
  133.7 4.5 %convert_reduce_fusion.6 = f32[128,4,8]{0,2,1:T(8,128)S(1)} fusion(f32[128,4,8]{0,2,1:T(8,128)S(1)} %select_maximum_fusion.4, f32[4,512,128,8]{2,1,3,0:T(8,128)} %get-tuple-element.359, pred[128,512]{0,1:T(8,128)(4,1)S(1)} %dynamic-slice_bitcast_fusion.4), kind=kLoop, calls=%fused_computation.3.clone.1 | loop fusion | flops 14675968 | bytes 8486912 | tf_op jit(solution)/shard_map/while/body/eval_jaxpr/reduce_sum | solution.py:50
  138.6 7.6 %bitcast_add_fusion.4 = f32[128,4,8,128]{0,3,2,1:T(8,128)} fusion(f32[128,4,8,128]{0,3,2,1:T(8,128)} %get-tuple-element.422, f32[128,4,8]{0,2,1:T(8,128)S(1)} %get-tuple-element.361, pred[]{:T(512)S(6)} %compare.6, bf16[1,512,4,128]{1,3,2,0:T(8,128)(2,1)S(1)} %copy.72, f32[4,512,128,8]{2,1,3,0:T(8,128)} %get-tuple-element.359, ...), kind=kOutput, calls=%fused_computation.6.clone.1 | convolution fusion | flops 548929536 | bytes 13205505 | tf_op jit(solution)/shard_map/while/body/eval_jaxpr/unqy,ynx->unqx/dot_general | solution.py:51
  146.2 6.9 %reshape_reshape.6 = bf16[8,512,4,128]{3,2,1,0:T(4,128)(2,1)} reshape(bf16[16,2,128,512]{3,2,1,0:T(8,128)(2,1)} %all-to-all-done.1) | data formatting | bytes 8388608 | tf_op jit(solution)/shard_map/reshape;reshape | solution.py:30
  153.1 18.5 %all-to-all-done.2 = bf16[16,2,128,512]{3,2,1,0:T(8,128)(2,1)} async-done(((bf16[16,2,128,512]{3,2,1,0:T(8,128)(2,1)}), bf16[16,2,128,512]{3,2,1,0:T(8,128)(2,1)}, u32[]{:S(2)}, u32[]{:S(2)}) %all-to-all-start.2) | async-done | bytes 4194336 | tf_op jit(solution)/shard_map/all_to_all | solution.py:99
  171.6 6.9 %reshape_reshape.7 = bf16[8,512,4,128]{3,2,1,0:T(4,128)(2,1)} reshape(bf16[16,2,128,512]{3,2,1,0:T(8,128)(2,1)} %all-to-all-done.2) | data formatting | bytes 8388608 | tf_op jit(solution)/shard_map/reshape;reshape | solution.py:31
  178.6 162.6 %while.31 = (s32[]{:T(128)}, f32[128,4,8]{0,2,1:T(8,128)S(1)}, f32[128,4,8]{0,2,1:T(8,128)S(1)}, f32[128,4,8,128]{0,3,2,1:T(8,128)}, pred[8,1,512]{2,1,0:T(4,128...) while((s32[]{:T(128)}, f32[128,4,8]{0,2,1:T(8,128)S(1)}, ...), condition=%wide.region_10.11_spmd.clone, body=%wide.region_7.10_spmd.clone.sunk | while | flops 1096306688 | bytes 51628208 | solution.py:56
  178.6 2.3 constant_dynamic-slice_fusion.7
  180.9 4.6 %bitcast_reduce_fusion.2 = (f32[128,4,8]{0,2,1:T(8,128)S(1)}, f32[4,512,128,8]{2,1,3,0:T(8,128)}) fusion(pred[512]{0:T(512)(128)(4,1)S(1)} %dynamic-slice_reduce_fusion.2, bf16[128,4,8,128]{3,0,2,1:T(8,128)(2,1)S(1)} %get-tuple-element.405, bf16[1,512,4,128]{3,2,1,0:T(4,128)(2,1)S(1)} %get-tuple-element.371), kind=kOutput, calls=%fused_computation.19.clone.1 | convolution fusion | flops 543158272 | bytes 9978368 | tf_op jit(solution)/shard_map/while/body/eval_jaxpr/swxl,cwl->swxc/dot_general | solution.py:38
  185.5 6.4 %convert_reduce_fusion.7 = (f32[128,4,8]{0,2,1:T(8,128)S(1)}, bf16[128,4,8,512]{0,3,2,1:T(8,128)(2,1)}) fusion(f32[128,4,8]{0,2,1:T(8,128)S(1)} %select_maximum_fusion.5, f32[4,512,128,8]{2,1,3,0:T(8,128)} %get-tuple-element.373, pred[512]{0:T(512)(128)(4,1)S(1)} %dynamic-slice_reduce_fusion.2), kind=kLoop, calls=%fused_computation.23.clone.1 | loop fusion | flops 14675968 | bytes 12616192 | tf_op jit(solution)/shard_map/while/body/eval_jaxpr/reduce_sum | solution.py:50
  191.9 2.1 copy.74
  194.0 3.5 bitcast_add_fusion.5
  198.9 2.3 constant_dynamic-slice_fusion.7
  201.2 4.6 %bitcast_reduce_fusion.2 = (f32[128,4,8]{0,2,1:T(8,128)S(1)}, f32[4,512,128,8]{2,1,3,0:T(8,128)}) fusion(pred[512]{0:T(512)(128)(4,1)S(1)} %dynamic-slice_reduce_fusion.2, bf16[128,4,8,128]{3,0,2,1:T(8,128)(2,1)S(1)} %get-tuple-element.405, bf16[1,512,4,128]{3,2,1,0:T(4,128)(2,1)S(1)} %get-tuple-element.371), kind=kOutput, calls=%fused_computation.19.clone.1 | convolution fusion | flops 543158272 | bytes 9978368 | tf_op jit(solution)/shard_map/while/body/eval_jaxpr/swxl,cwl->swxc/dot_general | solution.py:38
  205.8 6.4 %convert_reduce_fusion.7 = (f32[128,4,8]{0,2,1:T(8,128)S(1)}, bf16[128,4,8,512]{0,3,2,1:T(8,128)(2,1)}) fusion(f32[128,4,8]{0,2,1:T(8,128)S(1)} %select_maximum_fusion.5, f32[4,512,128,8]{2,1,3,0:T(8,128)} %get-tuple-element.373, pred[512]{0:T(512)(128)(4,1)S(1)} %dynamic-slice_reduce_fusion.2), kind=kLoop, calls=%fused_computation.23.clone.1 | loop fusion | flops 14675968 | bytes 12616192 | tf_op jit(solution)/shard_map/while/body/eval_jaxpr/reduce_sum | solution.py:50
  212.2 2.1 copy.74
  214.3 3.5 bitcast_add_fusion.5
  219.2 2.3 constant_dynamic-slice_fusion.7
  221.6 4.6 %bitcast_reduce_fusion.2 = (f32[128,4,8]{0,2,1:T(8,128)S(1)}, f32[4,512,128,8]{2,1,3,0:T(8,128)}) fusion(pred[512]{0:T(512)(128)(4,1)S(1)} %dynamic-slice_reduce_fusion.2, bf16[128,4,8,128]{3,0,2,1:T(8,128)(2,1)S(1)} %get-tuple-element.405, bf16[1,512,4,128]{3,2,1,0:T(4,128)(2,1)S(1)} %get-tuple-element.371), kind=kOutput, calls=%fused_computation.19.clone.1 | convolution fusion | flops 543158272 | bytes 9978368 | tf_op jit(solution)/shard_map/while/body/eval_jaxpr/swxl,cwl->swxc/dot_general | solution.py:38
  226.1 6.4 %convert_reduce_fusion.7 = (f32[128,4,8]{0,2,1:T(8,128)S(1)}, bf16[128,4,8,512]{0,3,2,1:T(8,128)(2,1)}) fusion(f32[128,4,8]{0,2,1:T(8,128)S(1)} %select_maximum_fusion.5, f32[4,512,128,8]{2,1,3,0:T(8,128)} %get-tuple-element.373, pred[512]{0:T(512)(128)(4,1)S(1)} %dynamic-slice_reduce_fusion.2), kind=kLoop, calls=%fused_computation.23.clone.1 | loop fusion | flops 14675968 | bytes 12616192 | tf_op jit(solution)/shard_map/while/body/eval_jaxpr/reduce_sum | solution.py:50
  232.6 2.1 copy.74
  234.7 3.5 bitcast_add_fusion.5
  239.5 2.3 constant_dynamic-slice_fusion.7
  241.9 4.6 %bitcast_reduce_fusion.2 = (f32[128,4,8]{0,2,1:T(8,128)S(1)}, f32[4,512,128,8]{2,1,3,0:T(8,128)}) fusion(pred[512]{0:T(512)(128)(4,1)S(1)} %dynamic-slice_reduce_fusion.2, bf16[128,4,8,128]{3,0,2,1:T(8,128)(2,1)S(1)} %get-tuple-element.405, bf16[1,512,4,128]{3,2,1,0:T(4,128)(2,1)S(1)} %get-tuple-element.371), kind=kOutput, calls=%fused_computation.19.clone.1 | convolution fusion | flops 543158272 | bytes 9978368 | tf_op jit(solution)/shard_map/while/body/eval_jaxpr/swxl,cwl->swxc/dot_general | solution.py:38
  246.5 6.4 %convert_reduce_fusion.7 = (f32[128,4,8]{0,2,1:T(8,128)S(1)}, bf16[128,4,8,512]{0,3,2,1:T(8,128)(2,1)}) fusion(f32[128,4,8]{0,2,1:T(8,128)S(1)} %select_maximum_fusion.5, f32[4,512,128,8]{2,1,3,0:T(8,128)} %get-tuple-element.373, pred[512]{0:T(512)(128)(4,1)S(1)} %dynamic-slice_reduce_fusion.2), kind=kLoop, calls=%fused_computation.23.clone.1 | loop fusion | flops 14675968 | bytes 12616192 | tf_op jit(solution)/shard_map/while/body/eval_jaxpr/reduce_sum | solution.py:50
  252.9 2.1 copy.74
  255.0 3.5 bitcast_add_fusion.5
  259.8 2.3 constant_dynamic-slice_fusion.7
  262.2 4.6 %bitcast_reduce_fusion.2 = (f32[128,4,8]{0,2,1:T(8,128)S(1)}, f32[4,512,128,8]{2,1,3,0:T(8,128)}) fusion(pred[512]{0:T(512)(128)(4,1)S(1)} %dynamic-slice_reduce_fusion.2, bf16[128,4,8,128]{3,0,2,1:T(8,128)(2,1)S(1)} %get-tuple-element.405, bf16[1,512,4,128]{3,2,1,0:T(4,128)(2,1)S(1)} %get-tuple-element.371), kind=kOutput, calls=%fused_computation.19.clone.1 | convolution fusion | flops 543158272 | bytes 9978368 | tf_op jit(solution)/shard_map/while/body/eval_jaxpr/swxl,cwl->swxc/dot_general | solution.py:38
  266.8 6.4 %convert_reduce_fusion.7 = (f32[128,4,8]{0,2,1:T(8,128)S(1)}, bf16[128,4,8,512]{0,3,2,1:T(8,128)(2,1)}) fusion(f32[128,4,8]{0,2,1:T(8,128)S(1)} %select_maximum_fusion.5, f32[4,512,128,8]{2,1,3,0:T(8,128)} %get-tuple-element.373, pred[512]{0:T(512)(128)(4,1)S(1)} %dynamic-slice_reduce_fusion.2), kind=kLoop, calls=%fused_computation.23.clone.1 | loop fusion | flops 14675968 | bytes 12616192 | tf_op jit(solution)/shard_map/while/body/eval_jaxpr/reduce_sum | solution.py:50
  273.2 2.1 copy.74
  275.3 3.5 bitcast_add_fusion.5
  280.2 2.3 constant_dynamic-slice_fusion.7
  282.5 4.6 %bitcast_reduce_fusion.2 = (f32[128,4,8]{0,2,1:T(8,128)S(1)}, f32[4,512,128,8]{2,1,3,0:T(8,128)}) fusion(pred[512]{0:T(512)(128)(4,1)S(1)} %dynamic-slice_reduce_fusion.2, bf16[128,4,8,128]{3,0,2,1:T(8,128)(2,1)S(1)} %get-tuple-element.405, bf16[1,512,4,128]{3,2,1,0:T(4,128)(2,1)S(1)} %get-tuple-element.371), kind=kOutput, calls=%fused_computation.19.clone.1 | convolution fusion | flops 543158272 | bytes 9978368 | tf_op jit(solution)/shard_map/while/body/eval_jaxpr/swxl,cwl->swxc/dot_general | solution.py:38
  287.1 6.4 %convert_reduce_fusion.7 = (f32[128,4,8]{0,2,1:T(8,128)S(1)}, bf16[128,4,8,512]{0,3,2,1:T(8,128)(2,1)}) fusion(f32[128,4,8]{0,2,1:T(8,128)S(1)} %select_maximum_fusion.5, f32[4,512,128,8]{2,1,3,0:T(8,128)} %get-tuple-element.373, pred[512]{0:T(512)(128)(4,1)S(1)} %dynamic-slice_reduce_fusion.2), kind=kLoop, calls=%fused_computation.23.clone.1 | loop fusion | flops 14675968 | bytes 12616192 | tf_op jit(solution)/shard_map/while/body/eval_jaxpr/reduce_sum | solution.py:50
  293.5 2.1 copy.74
  295.6 3.5 bitcast_add_fusion.5
  300.5 2.3 constant_dynamic-slice_fusion.7
  302.8 4.6 %bitcast_reduce_fusion.2 = (f32[128,4,8]{0,2,1:T(8,128)S(1)}, f32[4,512,128,8]{2,1,3,0:T(8,128)}) fusion(pred[512]{0:T(512)(128)(4,1)S(1)} %dynamic-slice_reduce_fusion.2, bf16[128,4,8,128]{3,0,2,1:T(8,128)(2,1)S(1)} %get-tuple-element.405, bf16[1,512,4,128]{3,2,1,0:T(4,128)(2,1)S(1)} %get-tuple-element.371), kind=kOutput, calls=%fused_computation.19.clone.1 | convolution fusion | flops 543158272 | bytes 9978368 | tf_op jit(solution)/shard_map/while/body/eval_jaxpr/swxl,cwl->swxc/dot_general | solution.py:38
  307.4 6.4 %convert_reduce_fusion.7 = (f32[128,4,8]{0,2,1:T(8,128)S(1)}, bf16[128,4,8,512]{0,3,2,1:T(8,128)(2,1)}) fusion(f32[128,4,8]{0,2,1:T(8,128)S(1)} %select_maximum_fusion.5, f32[4,512,128,8]{2,1,3,0:T(8,128)} %get-tuple-element.373, pred[512]{0:T(512)(128)(4,1)S(1)} %dynamic-slice_reduce_fusion.2), kind=kLoop, calls=%fused_computation.23.clone.1 | loop fusion | flops 14675968 | bytes 12616192 | tf_op jit(solution)/shard_map/while/body/eval_jaxpr/reduce_sum | solution.py:50
  313.8 2.1 copy.74
  315.9 3.5 bitcast_add_fusion.5
  320.8 2.3 constant_dynamic-slice_fusion.7
  323.2 4.6 %bitcast_reduce_fusion.2 = (f32[128,4,8]{0,2,1:T(8,128)S(1)}, f32[4,512,128,8]{2,1,3,0:T(8,128)}) fusion(pred[512]{0:T(512)(128)(4,1)S(1)} %dynamic-slice_reduce_fusion.2, bf16[128,4,8,128]{3,0,2,1:T(8,128)(2,1)S(1)} %get-tuple-element.405, bf16[1,512,4,128]{3,2,1,0:T(4,128)(2,1)S(1)} %get-tuple-element.371), kind=kOutput, calls=%fused_computation.19.clone.1 | convolution fusion | flops 543158272 | bytes 9978368 | tf_op jit(solution)/shard_map/while/body/eval_jaxpr/swxl,cwl->swxc/dot_general | solution.py:38
  327.7 6.4 %convert_reduce_fusion.7 = (f32[128,4,8]{0,2,1:T(8,128)S(1)}, bf16[128,4,8,512]{0,3,2,1:T(8,128)(2,1)}) fusion(f32[128,4,8]{0,2,1:T(8,128)S(1)} %select_maximum_fusion.5, f32[4,512,128,8]{2,1,3,0:T(8,128)} %get-tuple-element.373, pred[512]{0:T(512)(128)(4,1)S(1)} %dynamic-slice_reduce_fusion.2), kind=kLoop, calls=%fused_computation.23.clone.1 | loop fusion | flops 14675968 | bytes 12616192 | tf_op jit(solution)/shard_map/while/body/eval_jaxpr/reduce_sum | solution.py:50
  334.2 2.1 copy.74
  336.3 3.5 bitcast_add_fusion.5
  341.1 4.5 %add_divide_fusion = f32[128,4,8,128]{0,3,2,1:T(8,128)} fusion(f32[128,4,8,128]{0,3,2,1:T(8,128)} %get-tuple-element.96, f32[128,4,8,128]{0,3,2,1:T(8,128)} %get-tuple-element.93, f32[128,4,8]{0,2,1:T(8,128)S(1)} %get-tuple-element.239, f32[128,4,8]{0,2,1:T(8,128)S(1)} %get-tuple-element.241, f32[128,4,8]{0,2,1:T(8,128)S(1)} %get-tuple-element.240), kind=kLoop, calls=%fused_computation.37 | loop fusion | flops 2097152 | bytes 6340608 | tf_op jit(solution)/shard_map/div | solution.py:117
  345.6 2.9 copy.54
  (111 shorter events, 20.5 us)
Async XLA Ops:
  6.5 11.3 %copy-start = (bf16[24,128,512]{2,1,0:T(8,128)(2,1)S(1)}, bf16[24,128,512]{2,1,0:T(8,128)(2,1)}, u32[]{:S(2)}) copy-start(bf16[24,128,512]{2,1,0:T(8,128)(2,1)} %param.14) | copy-start | bytes 9437188
  8.6 21.7 %all-to-all-start = ((bf16[8,1,128,512]{3,2,1,0:T(8,128)(2,1)}), bf16[8,1,128,512]{3,2,1,0:T(8,128)(2,1)}, u32[]{:S(2)}, u32[]{:S(2)}) async-start(bf16[8,1,128,512]{3,2,1,0:T(8,128)(2,1)} %stack.2), calls=%async_computation | async-start | bytes 2097152 | tf_op jit(solution)/shard_map/all_to_all | solution.py:19
  30.3 7.2 %copy-start.4 = (bf16[24,128,512]{2,1,0:T(8,128)(2,1)S(1)}, bf16[24,128,512]{2,1,0:T(8,128)(2,1)}, u32[]{:S(2)}) copy-start(bf16[24,128,512]{2,1,0:T(8,128)(2,1)} %param.15) | copy-start | bytes 9437188
  30.3 74.1 %all-to-all-start.1 = ((bf16[16,2,128,512]{3,2,1,0:T(8,128)(2,1)}), bf16[16,2,128,512]{3,2,1,0:T(8,128)(2,1)}, u32[]{:S(2)}, u32[]{:S(2)}) async-start(bf16[16,2,128,512]{3,2,1,0:T(8,128)(2,1)} %bitcast.104), calls=%async_computation.1 | async-start | bytes 8388608 | tf_op jit(solution)/shard_map/all_to_all | solution.py:98
  36.4 52.3 %all-gather.2.cloned.1.call-start = ((), (), s32[]{:S(2)}) async-start(), calls=%async_computation.3 | async-start | bytes 1179648 | tf_op jit(solution)/shard_map/all_gather | solution.py:92
  104.4 67.3 %all-to-all-start.2 = ((bf16[16,2,128,512]{3,2,1,0:T(8,128)(2,1)}), bf16[16,2,128,512]{3,2,1,0:T(8,128)(2,1)}, u32[]{:S(2)}, u32[]{:S(2)}) async-start(bf16[16,2,128,512]{3,2,1,0:T(8,128)(2,1)} %bitcast.103), calls=%async_computation.2 | async-start | bytes 8388608 | tf_op jit(solution)/shard_map/all_to_all | solution.py:99
  185.5 8.5 %copy-start.2 = (f32[128,4,8,128]{0,3,2,1:T(8,128)S(1)}, f32[128,4,8,128]{0,3,2,1:T(8,128)}, u32[]{:S(2)}) copy-start(f32[128,4,8,128]{0,3,2,1:T(8,128)} %get-tuple-element.392) | copy-start | bytes 6291460 | tf_op jit(solution)/shard_map/while
  197.6 1.3 copy-start.3
  205.8 8.5 %copy-start.2 = (f32[128,4,8,128]{0,3,2,1:T(8,128)S(1)}, f32[128,4,8,128]{0,3,2,1:T(8,128)}, u32[]{:S(2)}) copy-start(f32[128,4,8,128]{0,3,2,1:T(8,128)} %get-tuple-element.392) | copy-start | bytes 6291460 | tf_op jit(solution)/shard_map/while
  217.9 1.3 copy-start.3
  226.1 8.5 %copy-start.2 = (f32[128,4,8,128]{0,3,2,1:T(8,128)S(1)}, f32[128,4,8,128]{0,3,2,1:T(8,128)}, u32[]{:S(2)}) copy-start(f32[128,4,8,128]{0,3,2,1:T(8,128)} %get-tuple-element.392) | copy-start | bytes 6291460 | tf_op jit(solution)/shard_map/while
  238.2 1.3 copy-start.3
  246.5 8.5 %copy-start.2 = (f32[128,4,8,128]{0,3,2,1:T(8,128)S(1)}, f32[128,4,8,128]{0,3,2,1:T(8,128)}, u32[]{:S(2)}) copy-start(f32[128,4,8,128]{0,3,2,1:T(8,128)} %get-tuple-element.392) | copy-start | bytes 6291460 | tf_op jit(solution)/shard_map/while
  258.5 1.3 copy-start.3
  266.8 8.5 %copy-start.2 = (f32[128,4,8,128]{0,3,2,1:T(8,128)S(1)}, f32[128,4,8,128]{0,3,2,1:T(8,128)}, u32[]{:S(2)}) copy-start(f32[128,4,8,128]{0,3,2,1:T(8,128)} %get-tuple-element.392) | copy-start | bytes 6291460 | tf_op jit(solution)/shard_map/while
  278.8 1.3 copy-start.3
  287.1 8.5 %copy-start.2 = (f32[128,4,8,128]{0,3,2,1:T(8,128)S(1)}, f32[128,4,8,128]{0,3,2,1:T(8,128)}, u32[]{:S(2)}) copy-start(f32[128,4,8,128]{0,3,2,1:T(8,128)} %get-tuple-element.392) | copy-start | bytes 6291460 | tf_op jit(solution)/shard_map/while
  299.2 1.3 copy-start.3
  307.4 8.5 %copy-start.2 = (f32[128,4,8,128]{0,3,2,1:T(8,128)S(1)}, f32[128,4,8,128]{0,3,2,1:T(8,128)}, u32[]{:S(2)}) copy-start(f32[128,4,8,128]{0,3,2,1:T(8,128)} %get-tuple-element.392) | copy-start | bytes 6291460 | tf_op jit(solution)/shard_map/while
  319.5 1.3 copy-start.3
  327.7 8.5 %copy-start.2 = (f32[128,4,8,128]{0,3,2,1:T(8,128)S(1)}, f32[128,4,8,128]{0,3,2,1:T(8,128)}, u32[]{:S(2)}) copy-start(f32[128,4,8,128]{0,3,2,1:T(8,128)} %get-tuple-element.392) | copy-start | bytes 6291460 | tf_op jit(solution)/shard_map/while
  339.8 1.3 copy-start.3
  341.1 7.4 %copy-start.1 = (bf16[24,128,512]{2,1,0:T(8,128)(2,1)S(1)}, bf16[24,128,512]{2,1,0:T(8,128)(2,1)}, u32[]{:S(2)}) copy-start(bf16[24,128,512]{2,1,0:T(8,128)(2,1)} %param.14) | copy-start | bytes 9437188
Sparse Core Ops, SparseCore 0:
  39.6 49.1 all-gather.1
